TPU v7x, 128 devices: a whole 4x4x4 slice. The times are simulated.
128 devices in a mesh: span: 32 (over x, z, y_lo), ctx: 4 (over y_hi, core).
Axes of the slice: x: 4, y: 4 (y_hi: 2, y_lo: 2; y = y_hi * 2 + y_lo), z: 4, core: 2. Of those that a mesh axis runs over, the one named last changes fastest.
Arguments:
- queries: bfloat16 [16384, 3072], P(('span', 'ctx')), may hold values from -64 to 64
- keys: bfloat16 [16384, 512], P(('span', 'ctx')), may hold values from -16 to 16
- values: bfloat16 [16384, 512], P(('span', 'ctx')), may hold values from -6 to 6
- temps: float32 [8, 24], replicated, may hold values from 0.5 to 2
- levels: int32 [32], replicated, may hold values from 0 to 7
- ctx_list: int32 [32, 4], replicated, may hold values from -1 to 30, as said below
- counts: int32 [32], replicated, may hold values from 256 to 512
Outputs:
- attended: bfloat16 [16384, 3072], P(('span', 'ctx'))
Inputs may be any that keep to these rules, and one draw needn't show every extreme that they name: `ctx_list`: slot 0 of span c's list is c - 1 (-1 for span 0). Slot 1, when used, is span 0. The other slots hold distinct spans below c - 1, used slots first, then -1. The list of span 32 - 1 has no -1.
All inputs are finite; a program needn't handle non-finite values.
Results may differ from a plain program's by a relative error of at most 0.0041.
Values may be sent and summed in bfloat16 or wider, within the bound.
A program may use at most 128 MiB of HBM per device.

v0:
```python
import math

import jax
import jax.numpy as jnp
from jax import lax
from jax.sharding import PartitionSpec as P

HQ = 24
KVH = 4
HD = 128


def slot_scores(query_group, key_slot, scale_group):
    scores = jnp.einsum("rgd,kd->grk", query_group, key_slot, preferred_element_type=jnp.float32)
    return scores * scale_group[:, None, None]


def row_maxima(query_rows, key_slots, mask, scale):
    group_size = HQ // KVH
    row_count = query_rows.shape[0]
    query_heads = query_rows.reshape(row_count, HQ, HD)
    maxima = []
    for kv_head in range(KVH):
        lower = kv_head * group_size
        query_group = query_heads[:, lower : lower + group_size]
        highest = jnp.full((group_size, row_count), -1e30, jnp.float32)
        for slot_index in range(key_slots.shape[0]):
            scores = slot_scores(
                query_group,
                key_slots[slot_index][:, kv_head * HD : (kv_head + 1) * HD],
                scale[lower : lower + group_size],
            )
            scores = jnp.where(mask[slot_index][None, None, :], scores, -1e30)
            highest = jnp.maximum(highest, jnp.max(scores, axis=-1))
        maxima.append(highest)
    return jnp.concatenate(maxima, axis=0)


def weighted_sums(query_rows, key_slots, value_slots, mask, scale, maxima):
    group_size = HQ // KVH
    row_count = query_rows.shape[0]
    query_heads = query_rows.reshape(row_count, HQ, HD)
    sums_list = []
    totals_list = []
    for kv_head in range(KVH):
        lower = kv_head * group_size
        query_group = query_heads[:, lower : lower + group_size]
        highest = maxima[lower : lower + group_size]
        accum = jnp.zeros((row_count, group_size, HD), jnp.float32)
        totals = jnp.zeros((group_size, row_count), jnp.float32)
        for slot_index in range(key_slots.shape[0]):
            scores = slot_scores(
                query_group,
                key_slots[slot_index][:, kv_head * HD : (kv_head + 1) * HD],
                scale[lower : lower + group_size],
            )
            keep = mask[slot_index][None, None, :]
            scores = jnp.where(keep, scores, -1e30)
            weights = jnp.where(keep, jnp.exp(scores - highest[:, :, None]), 0.0)
            totals = totals + jnp.sum(weights, axis=-1)
            value_group = value_slots[slot_index][:, kv_head * HD : (kv_head + 1) * HD]
            accum = accum + jnp.einsum(
                "grk,kd->rgd",
                weights.astype(jnp.bfloat16),
                value_group,
                preferred_element_type=jnp.float32,
            )
        sums_list.append(accum)
        totals_list.append(totals)
    sums = jnp.concatenate(sums_list, axis=1).reshape(row_count, HQ * HD)
    totals = jnp.transpose(jnp.concatenate(totals_list, axis=0))
    return (sums, totals)


def finish(sums, totals):
    row_count = sums.shape[0]
    result = sums.reshape(row_count, HQ, HD) / totals[:, :, None]
    return result.reshape(row_count, HQ * HD).astype(jnp.bfloat16)


def per_device(queries, keys, values, temps, levels, ctx_list, counts):
    span_index = lax.axis_index("span")
    tok_rows = keys.shape[0]
    width = keys.shape[1]
    wanted = lax.dynamic_index_in_dim(ctx_list, span_index, 0, keepdims=False)
    empty = jnp.zeros((wanted.shape[0], tok_rows, width), keys.dtype)
    piece_keys = lax.all_gather(keys, "span", axis=0, tiled=True)
    piece_values = lax.all_gather(values, "span", axis=0, tiled=True)
    length = piece_keys.shape[0]
    new_keys = []
    new_values = []
    for slot_index in range(wanted.shape[0]):
        source = wanted[slot_index]
        offset = source * tok_rows
        inside = (source >= 0) & (offset >= 0) & (offset + tok_rows <= length)
        begin = jnp.clip(offset, 0, length - tok_rows)
        slab_keys = lax.dynamic_slice_in_dim(piece_keys, begin, tok_rows, 0)
        slab_values = lax.dynamic_slice_in_dim(piece_values, begin, tok_rows, 0)
        new_keys.append(lax.select(inside, slab_keys, empty[slot_index]))
        new_values.append(lax.select(inside, slab_values, empty[slot_index]))
    context_keys = jnp.stack(new_keys)
    context_values = jnp.stack(new_values)
    slot_keys = jnp.concatenate([keys[None], context_keys], axis=0)
    slot_values = jnp.concatenate([values[None], context_values], axis=0)
    span_ids = jnp.concatenate([jnp.reshape(span_index, (1,)), wanted])
    valid_span = span_ids >= 0
    lengths = counts[jnp.maximum(span_ids, 0)]
    level = lax.dynamic_index_in_dim(levels, span_index, 0, keepdims=False)
    scale = lax.dynamic_index_in_dim(temps, level, 0, keepdims=False) / math.sqrt(HD)
    all_keys, all_values = (
        lax.all_gather(slot_keys, "ctx", axis=1, tiled=True),
        lax.all_gather(slot_values, "ctx", axis=1, tiled=True),
    )
    positions = jnp.arange(all_keys.shape[1], dtype=jnp.int32)
    mask = valid_span[:, None] & (positions[None, :] < lengths[:, None])
    maxima = row_maxima(queries, all_keys, mask, scale)
    sums, totals = weighted_sums(queries, all_keys, all_values, mask, scale, maxima)
    return finish(sums, totals)


def solution(mesh):
    return jax.shard_map(
        per_device,
        mesh=mesh,
        in_specs=(
            P(("span", "ctx"), None),
            P(("span", "ctx"), None),
            P(("span", "ctx"), None),
            P(),
            P(),
            P(),
            P(),
        ),
        out_specs=P(("span", "ctx"), None),
        check_vma=False,
    )
```

profile of v0, /device:TPU:1, one launch (start us, length us, event | category | flops | bytes accessed | tf_op | source)
XLA Modules:
  0.0 432.0 jit_solution(16926289602360051760)
XLA Ops:
  6.5 0.7 all-gather.9.cloned.1.call-update
  8.1 0.9 fusion.212
  14.5 0.9 bitcast_dynamic-update-slice_fusion.4
  15.4 0.9 bitcast_dynamic-update-slice_fusion.9
  16.3 133.3 %all-gather.9.cloned.1.call-done = bf16[4096,512]{1,0:T(8,128)(2,1)} async-done(((bf16[128,512]{1,0:T(8,128)(2,1)}), bf16[4096,512]{1,0:T(8,128)(2,1)}) %all-gather.9.cloned.1.call-update) | async-done | bytes 4194320 | tf_op jit(solution)/shard_map/all_gather | solution.py:87
  149.6 159.8 %all-gather.5.cloned.1.call-done = bf16[4096,512]{1,0:T(8,128)(2,1)} async-done(((bf16[128,512]{1,0:T(8,128)(2,1)}), bf16[4096,512]{1,0:T(8,128)(2,1)}) %all-gather.5.cloned.1.call-update) | async-done | bytes 4194320 | tf_op jit(solution)/shard_map/all_gather | solution.py:88
  309.5 1.1 bitcast_dynamic-update-slice_fusion.3
  310.5 1.0 bitcast_dynamic-update-slice_fusion.2
  311.5 1.0 bitcast_dynamic-update-slice_fusion.1
  312.5 1.0 bitcast_dynamic-update-slice_fusion
  313.4 0.8 copy-done.20
  318.3 0.7 fusion.190
  319.2 1.0 bitcast_dynamic-update-slice_fusion.7
  320.2 1.0 bitcast_dynamic-update-slice_fusion.6
  321.1 1.0 bitcast_dynamic-update-slice_fusion.5
  322.1 0.8 copy-done.21
  322.9 42.3 %all-gather.11.cloned.1.call-done = bf16[5,512,512]{2,1,0:T(8,128)(2,1)} async-done(((bf16[5,128,512]{2,1,0:T(8,128)(2,1)}), bf16[5,512,512]{2,1,0:T(8,128)(2,1)}) %all-gather.11.cloned.1.call-update) | async-done | bytes 2621456 | tf_op jit(solution)/shard_map/all_gather | solution.py:111
  365.3 1.9 slice_bitcast_fusion.7
  367.2 1.5 bitcast_reduce_fusion.19
  369.1 1.5 bitcast_reduce_fusion.18
  370.6 1.5 bitcast_reduce_fusion.17
  372.1 1.5 bitcast_reduce_fusion.16
  373.7 1.6 bitcast_reduce_fusion.15
  375.3 1.5 bitcast_reduce_fusion.13
  376.8 1.6 bitcast_reduce_fusion.12
  378.3 1.6 bitcast_reduce_fusion.11
  379.9 1.6 bitcast_reduce_fusion.10
  381.5 1.5 bitcast_reduce_fusion.9
  383.0 1.5 bitcast_reduce_fusion.8
  384.6 1.5 bitcast_reduce_fusion.4
  386.1 1.6 bitcast_reduce_fusion.3
  387.6 1.5 bitcast_reduce_fusion.7
  389.2 1.5 bitcast_reduce_fusion.2
  390.7 1.5 bitcast_reduce_fusion.6
  392.2 1.5 bitcast_reduce_fusion.1
  393.7 1.6 bitcast_reduce_fusion
  395.3 1.5 bitcast_reduce_fusion.5
  396.8 2.1 slice_bitcast_fusion
  399.5 0.8 copy-done.3
  401.5 0.8 copy-done.16
  403.5 0.7 copy-done.17
  407.2 3.4 fusion.73
  412.0 0.9 copy-done.4
  414.0 0.8 copy-done.6
  416.0 0.8 copy-done.1
  417.9 0.7 copy-done.9
  419.7 3.4 fusion.63
  424.3 1.2 copy.94
  (88 shorter events, 16.5 us)
Async XLA Ops:
  6.5 311.1 %copy-start = (s32[32]{0:T(128)S(1)}, s32[32]{0:T(128)}, u32[]{:S(2)}) copy-start(s32[32]{0:T(128)} %param.13) | copy-start | bytes 388
  6.5 307.8 %copy-start.23 = (s32[32]{0:T(128)S(1)}, s32[32]{0:T(128)}, u32[]{:S(2)}) copy-start(s32[32]{0:T(128)} %param.11) | copy-start | bytes 388
  6.5 309.9 %copy-start.22 = (bf16[128,3072]{1,0:T(8,128)(2,1)S(1)}, bf16[128,3072]{1,0:T(8,128)(2,1)}, u32[]{:S(2)}) copy-start(bf16[128,3072]{1,0:T(8,128)(2,1)} %param.7) | copy-start | bytes 2359300
  6.5 143.1 %all-gather.9.cloned.1.call-start = ((), (), s32[]{:S(2)}) async-start(), calls=%async_computation.2 | async-start | bytes 4325376 | tf_op jit(solution)/shard_map/all_gather | solution.py:87
  7.3 302.2 %all-gather.5.cloned.1.call-start = ((), (), s32[]{:S(2)}) async-start(), calls=%async_computation | async-start | bytes 4325376 | tf_op jit(solution)/shard_map/all_gather | solution.py:88
  8.0 357.2 %all-gather.11.cloned.1.call-start = ((), (), s32[]{:S(2)}) async-start(), calls=%async_computation.3 | async-start | bytes 3276800 | tf_op jit(solution)/shard_map/all_gather | solution.py:111
  313.4 0.8 copy-start.20
  314.3 82.6 %all-gather.7.cloned.1.call-start = ((), (), s32[]{:S(2)}) async-start(), calls=%async_computation.1 | async-start | bytes 3276800 | tf_op jit(solution)/shard_map/all_gather | solution.py:112
  322.1 0.8 copy-start.21
  396.8 2.2 copy-start.2
  398.9 1.4 copy-start.3
  399.5 1.5 copy-start.12
  400.8 1.5 copy-start.16
  401.5 1.5 copy-start.13
  402.7 1.5 copy-start.17
  403.5 1.5 copy-start.15
  404.7 1.5 copy-start.19
  405.0 1.6 copy-start.18
  405.5 1.7 copy-start.14
  411.5 1.4 copy-start.4
  412.0 1.5 copy-start.5
  413.4 1.4 copy-start.6
  414.0 1.5 copy-start.7
  415.3 1.5 copy-start.1
  415.9 1.5 copy-start.8
  417.2 1.5 copy-start.9
  417.5 1.6 copy-start.11
  417.9 1.8 copy-start.10
Sparse Core Ops, SparseCore 0:
  9.0 140.5 all-gather.8
  151.3 158.1 all-gather.4
  314.4 50.8 all-gather.10
  366.8 28.9 all-gather.6
where the time goes:
time: 433 us; the launch traced here: 432 us
  waiting for transfers between devices  337 us (78%)
  matrix products  38.6 us (9%)
  local copies, waits for them, and re-layouts  20.9 us (5%)
  between operations  20.7 us (5%)
  other arithmetic  14.8 us (3%)
    all_gather x1, waiting for transfers between devices, per_device(): piece_values = lax.all_gather(values, 'span', axis=0, tiled=True)  160 us
    all_gather x1, waiting for transfers between devices, per_device(): piece_keys = lax.all_gather(keys, 'span', axis=0, tiled=True)  133 us
    all_gather x1, waiting for transfers between devices, per_device(): lax.all_gather(slot_keys, 'ctx', axis=1, tiled=True)  42.3 us
    dot_general x20, matrix products, slot_scores(): jnp.einsum('rgd,kd->grk', query_group, key_slot, preferred_element_type=j...  29.6 us
    unnamed x51, local copies, waits for them, and re-layouts  12.9 us
    dot_general x20, matrix products, weighted_sums(): jnp.einsum('grk,kd->rgd', weights.astype(jnp.bfloat16), value_group, pref...  8.94 us
  transfers between devices with their start and end apart: 4, of which 3 were waited for; matrix products, arithmetic and copies ran while one was open for 9% of the time, Pallas kernels for 0%

commit v1 on v0

v1 whole, which is shorter than its diff:
```python
import functools
import math

import jax
import jax.numpy as jnp
from jax import lax
from jax.experimental import pallas as pl
from jax.experimental.pallas import tpu as pltpu
from jax.sharding import PartitionSpec as P

HQ = 24
KVH = 4
HD = 128
GROUP = HQ // KVH
WIDE = GROUP * HD
TOK = 512
PIECE = 128
SLOTS = 5
MESH = pl.DeviceIdType.MESH


def place():
    s = lax.axis_index("span")
    t = lax.axis_index("ctx")
    x = lax.div(s, 8)
    z = lax.rem(lax.div(s, 2), 4)
    y = lax.div(t, 2) * 2 + lax.rem(s, 2)
    core = lax.rem(t, 2)
    return s, t, x, z, y, core


def device(x, z, y, core):
    return ((x * 4 + z) * 2 + lax.rem(y, 2), lax.div(y, 2) * 2 + core)


def greet(targets):
    barrier = pltpu.get_barrier_semaphore()
    for target in targets:
        pl.semaphore_signal(barrier, inc=1, device_id=target, device_id_type=MESH)
    pl.semaphore_wait(barrier, len(targets))


def column_mates(x, z, y, core):
    flat = y * 2 + core
    mates = []
    for step in range(1, 8):
        other = lax.rem(flat + step, 8)
        mates.append(device(x, z, lax.div(other, 2), lax.rem(other, 2)))
    return mates


def gather_kernel(q_ref, k_ref, v_ref, g_ref, qa_ref, col_send, col_recv, ring_send, ring_recv, pair_send, pair_recv):
    s, t, x, z, y, core = place()
    yl = lax.rem(s, 2)

    def along(axis, step):
        moved = lax.rem((x if axis == 0 else z) + step + 4, 4)
        return device(moved, z, y, core) if axis == 0 else device(x, moved, y, core)

    greet(column_mates(x, z, y, core) + [along(axis, step) for axis in (0, 1) for step in (1, -1)])

    column = x * 4 + z
    sources = [k_ref, v_ref, q_ref]

    def landing(kind, parity, piece):
        rows = pl.ds(pl.multiple_of(piece * PIECE, PIECE), PIECE)
        if kind == 2:
            return qa_ref.at[rows, :]
        return g_ref.at[parity, kind, column, rows, :]

    def column_copy(kind, head):
        width = WIDE if kind == 2 else HD
        return pltpu.make_async_remote_copy(
            src_ref=sources[kind].at[:, pl.ds(head * width, width)],
            dst_ref=landing(kind, yl, t),
            send_sem=col_send.at[kind, head],
            recv_sem=col_recv.at[kind, t],
            device_id=device(x, z, head, yl),
            device_id_type=MESH,
        )

    def own_copy(kind, head):
        width = WIDE if kind == 2 else HD
        return pltpu.make_async_copy(
            sources[kind].at[:, pl.ds(head * width, width)], landing(kind, yl, t), col_recv.at[kind, t]
        )

    for kind in range(3):
        for head in range(KVH):
            mine = (y == head) & (core == yl)

            @pl.when(mine)
            def _():
                own_copy(kind, head).start()

            @pl.when(jnp.logical_not(mine))
            def _():
                column_copy(kind, head).start()

    def await_column(kind):
        for piece in range(4):
            spot = landing(kind, core, piece)
            pltpu.make_async_copy(spot, spot, col_recv.at[kind, piece]).wait()

    started = []

    def block_of(kv, da, db):
        first, second = (x, z) if kv == 0 else (z, x)
        first = lax.rem(first + da + 4, 4)
        second = lax.rem(second + db + 4, 4)
        return first * 4 + second if kv == 0 else second * 4 + first

    def rows_of(half):
        return pl.ds(0, TOK) if half is None else pl.ds(half * (TOK // 2), TOK // 2)

    def send(kv, da, db, half, leg, step):
        axis = leg if kv == 0 else 1 - leg
        block = block_of(kv, da, db)
        spot = g_ref.at[core, kv, block, rows_of(half), :]
        copy = pltpu.make_async_remote_copy(
            src_ref=spot,
            dst_ref=spot,
            send_sem=ring_send.at[len(started)],
            recv_sem=ring_recv.at[kv, block, half or 0],
            device_id=along(axis, step),
            device_id_type=MESH,
        )
        copy.start()
        started.append(copy)

    def arrive(kv, da, db, half):
        block = block_of(kv, da, db)
        spot = g_ref.at[core, kv, block, rows_of(half), :]
        pltpu.make_async_copy(spot, spot, ring_recv.at[kv, block, half or 0]).wait()

    paired = []

    def pair(kv, da, db):
        block = block_of(kv, da, db)
        spot = g_ref.at[core, kv, block]
        copy = pltpu.make_async_remote_copy(
            src_ref=spot,
            dst_ref=spot,
            send_sem=pair_send.at[len(paired)],
            recv_sem=pair_recv.at[kv, block],
            device_id=device(x, z, y, 1 - core),
            device_id_type=MESH,
        )
        copy.start()
        paired.append(copy)

    for kv in (0, 1):
        await_column(kv)
        for step in (1, -1):
            send(kv, 0, 0, None, 0, step)
    for kv in (0, 1):
        for step in (1, -1):
            send(kv, 0, 0, None, 1, step)
        pair(kv, 0, 0)
    for kv in (0, 1):
        arrive(kv, -1, 0, None)
        send(kv, -1, 0, 0, 0, 1)
        arrive(kv, 1, 0, None)
        send(kv, 1, 0, 1, 0, -1)
    for kv in (0, 1):
        for da in (-1, 1):
            for step in (1, -1):
                send(kv, da, 0, None, 1, step)
            pair(kv, da, 0)
    for kv in (0, 1):
        arrive(kv, 2, 0, 0)
        arrive(kv, 2, 0, 1)
        for step in (1, -1):
            send(kv, 2, 0, None, 1, step)
        pair(kv, 2, 0)
    for da in (0, -1, 1, 2):
        for kv in (0, 1):
            arrive(kv, da, -1, None)
            send(kv, da, -1, 0, 1, 1)
            pair(kv, da, -1)
            arrive(kv, da, 1, None)
            send(kv, da, 1, 1, 1, -1)
            pair(kv, da, 1)
    for da in (0, -1, 1, 2):
        for kv in (0, 1):
            arrive(kv, da, 2, 0)
            arrive(kv, da, 2, 1)
            pair(kv, da, 2)
    for kv in (0, 1):
        for block in range(16):
            spot = g_ref.at[1 - core, kv, block]
            pltpu.make_async_copy(spot, spot, pair_recv.at[kv, block]).wait()
    await_column(2)
    for kind in range(3):
        for head in range(KVH):

            @pl.when(jnp.logical_not((y == head) & (core == yl)))
            def _():
                column_copy(kind, head).wait_send()

    for copy in started + paired:
        copy.wait_send()


def gather(queries, keys, values):
    anywhere = pl.BlockSpec(memory_space=pl.ANY)
    return pl.pallas_call(
        gather_kernel,
        out_shape=(
            jax.ShapeDtypeStruct((2, 2, 16, TOK, HD), jnp.bfloat16),
            jax.ShapeDtypeStruct((TOK, WIDE), jnp.bfloat16),
        ),
        in_specs=[anywhere] * 3,
        out_specs=(anywhere, anywhere),
        scratch_shapes=[
            pltpu.SemaphoreType.DMA((3, 4)),
            pltpu.SemaphoreType.DMA((3, 4)),
            pltpu.SemaphoreType.DMA((40,)),
            pltpu.SemaphoreType.DMA((2, 16, 2)),
            pltpu.SemaphoreType.DMA((32,)),
            pltpu.SemaphoreType.DMA((2, 16)),
        ],
        compiler_params=pltpu.CompilerParams(collective_id=0, has_side_effects=True),
        name="gather_blocks",
    )(queries, keys, values)


def attend_kernel(temps, levels, ctx_list, counts, q_ref, g_ref, o_ref, kraw, vraw, kx, vx, sems):
    s, t, x, z, y, core = place()
    span = (x * 4 + z) * 2 + core
    ids = [span] + [ctx_list[span, j] for j in range(SLOTS - 1)]

    def fetch(slot):
        source = jnp.where(ids[slot] >= 0, ids[slot], span)
        parity, column = lax.rem(source, 2), lax.div(source, 2)
        return (
            pltpu.make_async_copy(g_ref.at[parity, 0, column], kraw.at[slot], sems.at[0, slot]),
            pltpu.make_async_copy(g_ref.at[parity, 1, column], vraw.at[slot], sems.at[1, slot]),
        )

    for slot in range(SLOTS):
        for copy in fetch(slot):
            copy.start()
    position = lax.broadcasted_iota(jnp.int32, (TOK, HD), 0)
    for slot in range(SLOTS):
        for copy in fetch(slot):
            copy.wait()
        source = jnp.where(ids[slot] >= 0, ids[slot], span)
        length = counts[source]
        rows = pl.ds(slot * TOK, TOK)
        key = kraw[slot].astype(jnp.float32)
        kx[rows, :] = jnp.where(position < length, key, key[0:1, :]).astype(jnp.bfloat16)
        used = jnp.where(ids[slot] >= 0, length, 0)
        value = vraw[slot].astype(jnp.float32)
        vx[rows, 0:HD] = jnp.where(position < used, value, 0.0).astype(jnp.bfloat16)
        vx[rows, HD : 2 * HD] = jnp.where(position < used, 1.0, 0.0).astype(jnp.bfloat16)
    level = levels[span]
    chunk = 256
    for head in range(GROUP):
        scale = temps[level, y * GROUP + head] * (math.log2(math.e) / math.sqrt(HD))
        for part in range(TOK // chunk):
            rows = pl.ds(part * chunk, chunk)
            cols = pl.ds(head * HD, HD)
            scores = lax.dot_general(
                q_ref[rows, cols], kx[...], (((1,), (1,)), ((), ())), preferred_element_type=jnp.float32
            )
            top = jnp.max(scores, axis=1, keepdims=True)
            weight = jnp.exp2((scores - top) * scale).astype(jnp.bfloat16)
            both = jnp.dot(weight, vx[...], preferred_element_type=jnp.float32)
            o_ref[rows, cols] = (both[:, 0:HD] / both[:, HD : 2 * HD]).astype(jnp.bfloat16)


def attend(temps, levels, ctx_list, counts, q_all, blocks):
    smem = pl.BlockSpec(memory_space=pltpu.SMEM)
    vmem = pl.BlockSpec(memory_space=pltpu.VMEM)
    return pl.pallas_call(
        attend_kernel,
        out_shape=jax.ShapeDtypeStruct((TOK, WIDE), jnp.bfloat16),
        in_specs=[smem] * 4 + [vmem, pl.BlockSpec(memory_space=pl.ANY)],
        out_specs=vmem,
        scratch_shapes=[
            pltpu.VMEM((SLOTS, TOK, HD), jnp.bfloat16),
            pltpu.VMEM((SLOTS, TOK, HD), jnp.bfloat16),
            pltpu.VMEM((SLOTS * TOK, HD), jnp.bfloat16),
            pltpu.VMEM((SLOTS * TOK, 2 * HD), jnp.bfloat16),
            pltpu.SemaphoreType.DMA((2, SLOTS)),
        ],
        compiler_params=pltpu.CompilerParams(vmem_limit_bytes=56 * 1024 * 1024),
        name="attend",
    )(temps, levels, ctx_list, counts, q_all, blocks)


def spread_kernel(o_ref, out_ref, send_sem, recv_sem):
    s, t, x, z, y, core = place()
    greet(column_mates(x, z, y, core))

    def owner(piece):
        return device(x, z, core + 2 * (piece // 2), piece % 2)

    def columns(head):
        return pl.ds(pl.multiple_of(head * WIDE, WIDE), WIDE)

    def remote(piece):
        return pltpu.make_async_remote_copy(
            src_ref=o_ref.at[pl.ds(piece * PIECE, PIECE), :],
            dst_ref=out_ref.at[:, columns(y)],
            send_sem=send_sem.at[piece],
            recv_sem=recv_sem.at[y],
            device_id=owner(piece),
            device_id_type=MESH,
        )

    def mine(piece):
        return (t == piece) & (lax.rem(s, 2) == core)

    for piece in range(4):

        @pl.when(mine(piece))
        def _():
            pltpu.make_async_copy(
                o_ref.at[pl.ds(piece * PIECE, PIECE), :], out_ref.at[:, columns(y)], recv_sem.at[y]
            ).start()

        @pl.when(jnp.logical_not(mine(piece)))
        def _():
            remote(piece).start()

    for head in range(KVH):
        spot = out_ref.at[:, columns(head)]
        pltpu.make_async_copy(spot, spot, recv_sem.at[head]).wait()
    for piece in range(4):

        @pl.when(jnp.logical_not(mine(piece)))
        def _():
            remote(piece).wait_send()


def spread(outputs):
    anywhere = pl.BlockSpec(memory_space=pl.ANY)
    return pl.pallas_call(
        spread_kernel,
        out_shape=jax.ShapeDtypeStruct((PIECE, HQ * HD), jnp.bfloat16),
        in_specs=[anywhere],
        out_specs=anywhere,
        scratch_shapes=[pltpu.SemaphoreType.DMA((4,)), pltpu.SemaphoreType.DMA((4,))],
        compiler_params=pltpu.CompilerParams(collective_id=1, has_side_effects=True),
        name="spread_outputs",
    )(outputs)


def per_device(queries, keys, values, temps, levels, ctx_list, counts):
    blocks, q_all = gather(queries, keys, values)
    outputs = attend(temps, levels, ctx_list, counts, q_all, blocks)
    return spread(outputs)


def solution(mesh):
    return jax.shard_map(
        per_device,
        mesh=mesh,
        in_specs=(
            P(("span", "ctx"), None),
            P(("span", "ctx"), None),
            P(("span", "ctx"), None),
            P(),
            P(),
            P(),
            P(),
        ),
        out_specs=P(("span", "ctx"), None),
        check_vma=False,
    )
```

time: 433 us -> 71.5 us (0.17)
  waiting for transfers between devices: 337 us -> 0 us
  Pallas kernels: 0 us -> 67.9 us
  matrix products: 38.6 us -> 0 us
  between operations: 20.7 us -> 0.03 us
  local copies, waits for them, and re-layouts: 20.9 us -> 3.42 us
  other arithmetic: 14.8 us -> 0 us
    all_gather x4 -> x0, waiting for transfers between devices: 335 us -> none  [the longest x1 160 us: per_device(): piece_values = lax.all_gather(values, 'span', axis=0, tiled=True)]
    pallas_call x0 -> x3, Pallas kernels: none -> 67.9 us  [the longest x1 41 us: gather(): pl.pallas_call(gather_kernel, out_shape=(jax.ShapeDtypeStruct((2, 2, 16,...]
    dot_general x40 -> x0, matrix products: 38.6 us -> none  [the longest x20 29.6 us: slot_scores(): jnp.einsum('rgd,kd->grk', query_group, key_slot, preferred_element_type=j...]
    unnamed x51 -> x2, local copies, waits for them, and re-layouts: 12.9 us -> 3.42 us
    reduce_sum x2 -> x0, other arithmetic: 6.82 us -> none  [weighted_sums(): totals = totals + jnp.sum(weights, axis=-1)]
    unnamed x5 -> x0, other arithmetic: 4.88 us -> none
  transfers between devices with their start and end apart: 4 -> 0, of which waited for: 3 -> 0; matrix products, arithmetic and copies ran while one was open for 9% -> 0% of each run, Pallas kernels for 0% -> 0%
where the time goes in v1:
time: 71.5 us; the launch traced here: 71.3 us
  Pallas kernels  67.9 us (95%)
  local copies, waits for them, and re-layouts  3.42 us (5%)
    pallas_call x1, Pallas kernels, gather(): pl.pallas_call(gather_kernel, out_shape=(jax.ShapeDtypeStruct((2, 2, 16,...  41 us
    pallas_call x1, Pallas kernels, spread(): pl.pallas_call(spread_kernel, out_shape=jax.ShapeDtypeStruct((PIECE, HQ *...  13.9 us
    pallas_call x1, Pallas kernels, attend(): pl.pallas_call(attend_kernel, out_shape=jax.ShapeDtypeStruct((TOK, WIDE),...  13 us
    unnamed x2, local copies, waits for them, and re-layouts  3.42 us

profile of v1, /device:TPU:1, one launch (start us, length us, event | category | flops | bytes accessed | tf_op | source)
XLA Modules:
  0.0 71.3 jit_solution(8534950415836996645)
XLA Ops:
  0.0 1.4 %copy.8.ctx_list = s32[32,4]{1,0:T(8,128)} copy(s32[32,4]{0,1:T(4,128)} %param.12) | data formatting | bytes 1024 | tf_op args[5]
  1.4 41.0 %gather_blocks.1 = (bf16[2,2,16,512,128]{4,3,2,1,0:T(8,128)(2,1)}, bf16[512,768]{1,0:T(8,128)(2,1)}) custom-call(bf16[128,3072]{1,0:T(8,128)(2,1)} %q_ref.1, bf16[128,512]{1,0:T(8,128)(2,1)} %k_ref.1, bf16[128,512]{1,0:T(8,128)(2,1)} %v_ref.1), custom_call_target="tpu_custom_call" | custom-call | tf_op jit(solution)/shard_map/gather_blocks/pallas_call | solution.py:207
  42.3 13.0 %attend.1.o_ref = bf16[512,768]{1,0:T(8,128)(2,1)} custom-call(f32[8,24]{1,0:T(8,128)} %temps.1, s32[32]{0:T(128)} %levels.1, s32[32,4]{1,0:T(8,128)} %copy.8.ctx_list, s32[32]{0:T(128)} %counts.1, bf16[512,768]{1,0:T(8,128)(2,1)} %get-tuple-element.7.q_ref, bf16[2,2,16,512,128]{4,3,2,1,0:T(8,128)(2,1)} %get-tuple-element.8.g_ref), custom_call_target="tpu_custom_call" | custom-call | tf_op jit(solution)/shard_map/attend/pallas_call | solution.py:276
  55.3 13.9 %spread_outputs.1 = bf16[128,3072]{1,0:T(8,128)(2,1)} custom-call(bf16[512,768]{1,0:T(8,128)(2,1)} %attend.1.o_ref), custom_call_target="tpu_custom_call" | custom-call | tf_op jit(solution)/shard_map/spread_outputs/pallas_call | solution.py:340
  69.2 2.1 %copy.10 = bf16[128,3072]{1,0:T(8,128)(2,1)} copy(bf16[128,3072]{1,0:T(8,128)(2,1)} %spread_outputs.1) | data formatting | bytes 1572864

commit v2 on v1

v2 whole, which is shorter than its diff:
```python
import functools
import math

import jax
import jax.numpy as jnp
from jax import lax
from jax.experimental import pallas as pl
from jax.experimental.pallas import tpu as pltpu
from jax.sharding import PartitionSpec as P

HQ = 24
KVH = 4
HD = 128
GROUP = HQ // KVH
WIDE = GROUP * HD
TOK = 512
PIECE = 128
SLOTS = 5
EARLY = 2
CHUNK = 256
MESH = pl.DeviceIdType.MESH


def place():
    s = lax.axis_index("span")
    t = lax.axis_index("ctx")
    x = lax.div(s, 8)
    z = lax.rem(lax.div(s, 2), 4)
    y = lax.div(t, 2) * 2 + lax.rem(s, 2)
    core = lax.rem(t, 2)
    return s, t, x, z, y, core


def device(x, z, y, core):
    return ((x * 4 + z) * 2 + lax.rem(y, 2), lax.div(y, 2) * 2 + core)


def greet(targets):
    barrier = pltpu.get_barrier_semaphore()
    for target in targets:
        pl.semaphore_signal(barrier, inc=1, device_id=target, device_id_type=MESH)
    pl.semaphore_wait(barrier, len(targets))


def column_mates(x, z, y, core):
    flat = y * 2 + core
    mates = []
    for step in range(1, 8):
        other = lax.rem(flat + step, 8)
        mates.append(device(x, z, lax.div(other, 2), lax.rem(other, 2)))
    return mates


def fused_kernel(
    temps, levels, ctx_t, counts, q_ref, k_ref, v_ref, out_ref,
    g_ref, qa_ref, kx, vx, acc_ref, top_ref, o_ref,
    col_send, col_recv, ring_send, ring_recv, pair_send, pair_recv, out_send, out_recv,
):
    s, t, x, z, y, core = place()
    yl = lax.rem(s, 2)
    column = x * 4 + z
    span = column * 2 + core

    def along(axis, step):
        moved = lax.rem((x if axis == 0 else z) + step + 4, 4)
        return device(moved, z, y, core) if axis == 0 else device(x, moved, y, core)

    greet(column_mates(x, z, y, core) + [along(axis, step) for axis in (0, 1) for step in (1, -1)])

    sources = [k_ref, v_ref, q_ref]

    def landing(kind, parity, piece):
        rows = pl.ds(pl.multiple_of(piece * PIECE, PIECE), PIECE)
        if kind == 2:
            return qa_ref.at[rows, :]
        return g_ref.at[parity, kind, column, rows, :]

    def column_copy(kind, head):
        width = WIDE if kind == 2 else HD
        return pltpu.make_async_remote_copy(
            src_ref=sources[kind].at[:, pl.ds(head * width, width)],
            dst_ref=landing(kind, yl, t),
            send_sem=col_send.at[kind, head],
            recv_sem=col_recv.at[kind, t],
            device_id=device(x, z, head, yl),
            device_id_type=MESH,
        )

    def own_copy(kind, head):
        width = WIDE if kind == 2 else HD
        return pltpu.make_async_copy(
            sources[kind].at[:, pl.ds(head * width, width)], landing(kind, yl, t), col_recv.at[kind, t]
        )

    for kind in range(3):
        for head in range(KVH):
            mine = (y == head) & (core == yl)

            @pl.when(mine)
            def _():
                own_copy(kind, head).start()

            @pl.when(jnp.logical_not(mine))
            def _():
                column_copy(kind, head).start()

    def await_column(kind):
        for piece in range(4):
            spot = landing(kind, core, piece)
            pltpu.make_async_copy(spot, spot, col_recv.at[kind, piece]).wait()

    started = []

    def block_of(kv, da, db):
        first, second = (x, z) if kv == 0 else (z, x)
        first = lax.rem(first + da + 4, 4)
        second = lax.rem(second + db + 4, 4)
        return first * 4 + second if kv == 0 else second * 4 + first

    def rows_of(half):
        return pl.ds(0, TOK) if half is None else pl.ds(half * (TOK // 2), TOK // 2)

    def send(kv, da, db, half, leg, step):
        axis = leg if kv == 0 else 1 - leg
        block = block_of(kv, da, db)
        spot = g_ref.at[core, kv, block, rows_of(half), :]
        copy = pltpu.make_async_remote_copy(
            src_ref=spot,
            dst_ref=spot,
            send_sem=ring_send.at[len(started)],
            recv_sem=ring_recv.at[kv, block, half or 0],
            device_id=along(axis, step),
            device_id_type=MESH,
        )
        copy.start()
        started.append(copy)

    def arrive(kv, da, db, half):
        block = block_of(kv, da, db)
        spot = g_ref.at[core, kv, block, rows_of(half), :]
        pltpu.make_async_copy(spot, spot, ring_recv.at[kv, block, half or 0]).wait()

    paired = []

    def pair(kv, da, db):
        block = block_of(kv, da, db)
        spot = g_ref.at[core, kv, block]
        copy = pltpu.make_async_remote_copy(
            src_ref=spot,
            dst_ref=spot,
            send_sem=pair_send.at[len(paired)],
            recv_sem=pair_recv.at[kv, block],
            device_id=device(x, z, y, 1 - core),
            device_id_type=MESH,
        )
        copy.start()
        paired.append(copy)

    def await_pair(kv, block):
        spot = g_ref.at[1 - core, kv, block]
        pltpu.make_async_copy(spot, spot, pair_recv.at[kv, block]).wait()

    position = lax.broadcasted_iota(jnp.int32, (TOK, HD), 0)

    def prepare(slot, source, used):
        parity, place_of = lax.rem(source, 2), lax.div(source, 2)
        length = counts[source]
        rows = pl.ds(slot * TOK, TOK)
        key = g_ref[parity, 0, place_of].astype(jnp.float32)
        kx[rows, :] = jnp.where(position < length, key, key[0:1, :]).astype(jnp.bfloat16)
        limit = jnp.where(used, length, 0)
        value = g_ref[parity, 1, place_of].astype(jnp.float32)
        vx[rows, 0:HD] = jnp.where(position < limit, value, 0.0).astype(jnp.bfloat16)
        vx[rows, HD : 2 * HD] = jnp.where(position < limit, 1.0, 0.0).astype(jnp.bfloat16)

    level = levels[span]

    def scale_of(head):
        return temps[level, y * GROUP + head] * (math.log2(math.e) / math.sqrt(HD))

    def scores_of(head, part, low, high):
        return lax.dot_general(
            qa_ref[pl.ds(part * CHUNK, CHUNK), pl.ds(head * HD, HD)],
            kx[pl.ds(low * TOK, (high - low) * TOK), :],
            (((1,), (1,)), ((), ())),
            preferred_element_type=jnp.float32,
        )

    def early(piece):
        head, part = piece // (TOK // CHUNK), piece % (TOK // CHUNK)
        rows = pl.ds(part * CHUNK, CHUNK)
        scores = scores_of(head, part, 0, EARLY)
        top = jnp.max(scores, axis=1, keepdims=True)
        weight = jnp.exp2((scores - top) * scale_of(head)).astype(jnp.bfloat16)
        top_ref[head, rows, :] = jnp.broadcast_to(top, (CHUNK, HD))
        acc_ref[head, rows, :] = jnp.dot(
            weight, vx[pl.ds(0, EARLY * TOK), :], preferred_element_type=jnp.float32
        )

    def late(head, part):
        rows = pl.ds(part * CHUNK, CHUNK)
        scale = scale_of(head)
        scores = scores_of(head, part, EARLY, SLOTS)
        before = top_ref[head, rows, 0:1]
        top = jnp.maximum(before, jnp.max(scores, axis=1, keepdims=True))
        weight = jnp.exp2((scores - top) * scale).astype(jnp.bfloat16)
        both = jnp.dot(
            weight, vx[pl.ds(EARLY * TOK, (SLOTS - EARLY) * TOK), :], preferred_element_type=jnp.float32
        )
        both = both + acc_ref[head, rows, :] * jnp.exp2((before - top) * scale)
        o_ref[rows, pl.ds(head * HD, HD)] = (both[:, 0:HD] / both[:, HD : 2 * HD]).astype(jnp.bfloat16)

    for kv in (0, 1):
        await_column(kv)
        for step in (1, -1):
            send(kv, 0, 0, None, 0, step)
    for kv in (0, 1):
        for step in (1, -1):
            send(kv, 0, 0, None, 1, step)
        pair(kv, 0, 0)
    for kv in (0, 1):
        arrive(kv, -1, 0, None)
        send(kv, -1, 0, 0, 0, 1)
        arrive(kv, 1, 0, None)
        send(kv, 1, 0, 1, 0, -1)
    for kv in (0, 1):
        for da in (-1, 1):
            for step in (1, -1):
                send(kv, da, 0, None, 1, step)
            pair(kv, da, 0)
    for kv in (0, 1):
        arrive(kv, 2, 0, 0)
        arrive(kv, 2, 0, 1)
        for step in (1, -1):
            send(kv, 2, 0, None, 1, step)
        pair(kv, 2, 0)
    prepare(0, span, True)
    await_column(2)

    def hop(kv, da):
        arrive(kv, da, -1, None)
        send(kv, da, -1, 0, 1, 1)
        pair(kv, da, -1)
        arrive(kv, da, 1, None)
        send(kv, da, 1, 1, 1, -1)
        pair(kv, da, 1)

    def last_hop(kv, da):
        arrive(kv, da, 2, 0)
        arrive(kv, da, 2, 1)
        pair(kv, da, 2)

    for da in (0, -1):
        for kv in (0, 1):
            hop(kv, da)
    near = lax.rem(column + core + 15, 16)
    for kv in (0, 1):
        await_pair(kv, near)
    prepare(1, lax.rem(span + 31, 32), span > 0)
    steps = [functools.partial(hop, kv, da) for da in (1, 2) for kv in (0, 1)]
    steps += [functools.partial(last_hop, kv, da) for da in (0, -1, 1, 2) for kv in (0, 1)]
    for piece, step in enumerate(steps):
        step()
        early(piece)
    for kv in (0, 1):
        for block in range(16):

            @pl.when(block != near)
            def _():
                await_pair(kv, block)

    for slot in range(EARLY, SLOTS):
        listed = ctx_t[slot - 1, span]
        prepare(slot, jnp.where(listed >= 0, listed, span), listed >= 0)

    def out_columns(role, head):
        return pl.ds(pl.multiple_of(role * WIDE + head * HD, HD), HD)

    def out_copy(head, piece):
        return pltpu.make_async_remote_copy(
            src_ref=o_ref.at[pl.ds(piece * PIECE, PIECE), pl.ds(head * HD, HD)],
            dst_ref=out_ref.at[:, out_columns(y, head)],
            send_sem=out_send.at[head, piece],
            recv_sem=out_recv.at[y, head],
            device_id=device(x, z, core + 2 * (piece // 2), piece % 2),
            device_id_type=MESH,
        )

    def kept(piece):
        return (t == piece) & (yl == core)

    def send_out(head):
        for piece in range(4):

            @pl.when(kept(piece))
            def _():
                pltpu.make_async_copy(
                    o_ref.at[pl.ds(piece * PIECE, PIECE), pl.ds(head * HD, HD)],
                    out_ref.at[:, out_columns(y, head)],
                    out_recv.at[y, head],
                ).start()

            @pl.when(jnp.logical_not(kept(piece)))
            def _():
                out_copy(head, piece).start()

    for head in range(GROUP):
        for part in range(TOK // CHUNK):
            late(head, part)
            if head > 0 and part == 0:
                send_out(head - 1)
    for kind in range(3):
        for head in range(KVH):

            @pl.when(jnp.logical_not((y == head) & (core == yl)))
            def _():
                column_copy(kind, head).wait_send()

    for copy in started + paired:
        copy.wait_send()
    send_out(GROUP - 1)
    for role in range(KVH):
        for head in range(GROUP):
            spot = out_ref.at[:, out_columns(role, head)]
            pltpu.make_async_copy(spot, spot, out_recv.at[role, head]).wait()
    for head in range(GROUP):
        for piece in range(4):

            @pl.when(jnp.logical_not(kept(piece)))
            def _():
                out_copy(head, piece).wait_send()


def per_device(queries, keys, values, temps, levels, ctx_list, counts):
    anywhere = pl.BlockSpec(memory_space=pl.ANY)
    smem = pl.BlockSpec(memory_space=pltpu.SMEM)
    dma = pltpu.SemaphoreType.DMA
    return pl.pallas_call(
        fused_kernel,
        out_shape=jax.ShapeDtypeStruct((PIECE, HQ * HD), jnp.bfloat16),
        in_specs=[smem] * 4 + [anywhere] * 3,
        out_specs=anywhere,
        scratch_shapes=[
            pltpu.VMEM((2, 2, 16, TOK, HD), jnp.bfloat16),
            pltpu.VMEM((TOK, WIDE), jnp.bfloat16),
            pltpu.VMEM((SLOTS * TOK, HD), jnp.bfloat16),
            pltpu.VMEM((SLOTS * TOK, 2 * HD), jnp.bfloat16),
            pltpu.VMEM((GROUP, TOK, 2 * HD), jnp.float32),
            pltpu.VMEM((GROUP, TOK, HD), jnp.float32),
            pltpu.VMEM((TOK, WIDE), jnp.bfloat16),
            dma((3, 4)),
            dma((3, 4)),
            dma((40,)),
            dma((2, 16, 2)),
            dma((32,)),
            dma((2, 16)),
            dma((GROUP, 4)),
            dma((KVH, GROUP)),
        ],
        compiler_params=pltpu.CompilerParams(
            collective_id=0, has_side_effects=True, vmem_limit_bytes=56 * 1024 * 1024
        ),
        name="span_attention",
    )(temps, levels, ctx_list.T, counts, queries, keys, values)


def solution(mesh):
    return jax.shard_map(
        per_device,
        mesh=mesh,
        in_specs=(
            P(("span", "ctx"), None),
            P(("span", "ctx"), None),
            P(("span", "ctx"), None),
            P(),
            P(),
            P(),
            P(),
        ),
        out_specs=P(("span", "ctx"), None),
        check_vma=False,
    )
```

time: 71.5 us -> 61.6 us (0.86)
  Pallas kernels: 67.9 us -> 59.3 us
  local copies, waits for them, and re-layouts: 3.42 us -> 2.06 us
    pallas_call x3 -> x1, Pallas kernels: 67.9 us -> 59.3 us  [per_device(): pl.pallas_call(fused_kernel, out_shape=jax.ShapeDtypeStruct((PIECE, HQ *...]
    unnamed x2 -> x1, local copies, waits for them, and re-layouts: 3.42 us -> 2.06 us
where the time goes in v2:
time: 61.6 us; the launch traced here: 61.4 us
  Pallas kernels  59.3 us (96%)
  local copies, waits for them, and re-layouts  2.06 us (3%)
    pallas_call x1, Pallas kernels, per_device(): pl.pallas_call(fused_kernel, out_shape=jax.ShapeDtypeStruct((PIECE, HQ *...  59.3 us
    unnamed x1, local copies, waits for them, and re-layouts  2.06 us

profile of v2, /device:TPU:1, one launch (start us, length us, event | category | flops | bytes accessed | tf_op | source)
XLA Modules:
  0.0 61.4 jit_solution(17306021740965712461)
XLA Ops:
  0.0 59.3 %span_attention.1 = bf16[128,3072]{1,0:T(8,128)(2,1)} custom-call(f32[8,24]{1,0:T(8,128)} %temps.1, s32[32]{0:T(128)} %levels.1, s32[4,32]{1,0:T(4,128)} %bitcast.1, s32[32]{0:T(128)} %counts.1, bf16[128,3072]{1,0:T(8,128)(2,1)} %q_ref.1, bf16[128,512]{1,0:T(8,128)(2,1)} %k_ref.1, bf16[128,512]{1,0:T(8,128)(2,1)} %v_ref.1), custom_call_target="tpu_custom_call" | custom-call | tf_op jit(solution)/shard_map/span_attention/pallas_call | solution.py:338
  59.3 2.1 %copy.9 = bf16[128,3072]{1,0:T(8,128)(2,1)} copy(bf16[128,3072]{1,0:T(8,128)(2,1)} %span_attention.1) | data formatting | bytes 1572864

commit v3 on v2

--- a/solution.py
+++ b/solution.py
@@ -104,10 +104,12 @@
             def _():
                 column_copy(kind, head).start()
 
-    def await_column(kind):
-        for piece in range(4):
-            spot = landing(kind, core, piece)
-            pltpu.make_async_copy(spot, spot, col_recv.at[kind, piece]).wait()
+    def await_piece(kind, piece):
+        spot = landing(kind, core, piece)
+        pltpu.make_async_copy(spot, spot, col_recv.at[kind, piece]).wait()
+
+    close = jnp.where(y - core == 2, 1, 0)
+    halves = (close, 1 - close)
 
     started = []
 
@@ -118,7 +120,7 @@
         return first * 4 + second if kv == 0 else second * 4 + first
 
     def rows_of(half):
-        return pl.ds(0, TOK) if half is None else pl.ds(half * (TOK // 2), TOK // 2)
+        return pl.ds(pl.multiple_of(halves[half] * (TOK // 2), TOK // 2), TOK // 2)
 
     def send(kv, da, db, half, leg, step):
         axis = leg if kv == 0 else 1 - leg
@@ -128,7 +130,7 @@
             src_ref=spot,
             dst_ref=spot,
             send_sem=ring_send.at[len(started)],
-            recv_sem=ring_recv.at[kv, block, half or 0],
+            recv_sem=ring_recv.at[kv, block, half],
             device_id=along(axis, step),
             device_id_type=MESH,
         )
@@ -138,7 +140,7 @@
     def arrive(kv, da, db, half):
         block = block_of(kv, da, db)
         spot = g_ref.at[core, kv, block, rows_of(half), :]
-        pltpu.make_async_copy(spot, spot, ring_recv.at[kv, block, half or 0]).wait()
+        pltpu.make_async_copy(spot, spot, ring_recv.at[kv, block, half]).wait()
 
     paired = []
 
@@ -211,38 +213,40 @@
         o_ref[rows, pl.ds(head * HD, HD)] = (both[:, 0:HD] / both[:, HD : 2 * HD]).astype(jnp.bfloat16)
 
     for kv in (0, 1):
-        await_column(kv)
-        for step in (1, -1):
-            send(kv, 0, 0, None, 0, step)
-    for kv in (0, 1):
-        for step in (1, -1):
-            send(kv, 0, 0, None, 1, step)
+        for half in (0, 1):
+            for row in (0, 1):
+                await_piece(kv, 2 * halves[half] + row)
+            for leg in (0, 1):
+                for step in (1, -1):
+                    send(kv, 0, 0, half, leg, step)
         pair(kv, 0, 0)
     for kv in (0, 1):
-        arrive(kv, -1, 0, None)
-        send(kv, -1, 0, 0, 0, 1)
-        arrive(kv, 1, 0, None)
-        send(kv, 1, 0, 1, 0, -1)
-    for kv in (0, 1):
-        for da in (-1, 1):
+        for half in (0, 1):
+            for da in (-1, 1):
+                arrive(kv, da, 0, half)
+                if half == (da + 1) // 2:
+                    send(kv, da, 0, half, 0, -da)
+                for step in (1, -1):
+                    send(kv, da, 0, half, 1, step)
+        pair(kv, -1, 0)
+        pair(kv, 1, 0)
+    for kv in (0, 1):
+        for half in (0, 1):
+            arrive(kv, 2, 0, half)
             for step in (1, -1):
-                send(kv, da, 0, None, 1, step)
-            pair(kv, da, 0)
-    for kv in (0, 1):
-        arrive(kv, 2, 0, 0)
-        arrive(kv, 2, 0, 1)
-        for step in (1, -1):
-            send(kv, 2, 0, None, 1, step)
+                send(kv, 2, 0, half, 1, step)
         pair(kv, 2, 0)
     prepare(0, span, True)
-    await_column(2)
+    for piece in range(4):
+        await_piece(2, piece)
 
     def hop(kv, da):
-        arrive(kv, da, -1, None)
-        send(kv, da, -1, 0, 1, 1)
+        for half in (0, 1):
+            for db in (-1, 1):
+                arrive(kv, da, db, half)
+                if half == (db + 1) // 2:
+                    send(kv, da, db, half, 1, -db)
         pair(kv, da, -1)
-        arrive(kv, da, 1, None)
-        send(kv, da, 1, 1, 1, -1)
         pair(kv, da, 1)
 
     def last_hop(kv, da):
@@ -350,7 +354,7 @@
             pltpu.VMEM((TOK, WIDE), jnp.bfloat16),
             dma((3, 4)),
             dma((3, 4)),
-            dma((40,)),
+            dma((60,)),
             dma((2, 16, 2)),
             dma((32,)),
             dma((2, 16)),

time: 61.6 us -> 61.5 us (level)
  no operation moved by 1% of the time
where the time goes in v3:
time: 61.5 us; the launch traced here: 61.4 us
  Pallas kernels  59.3 us (96%)
  local copies, waits for them, and re-layouts  2.06 us (3%)
    pallas_call x1, Pallas kernels, per_device(): pl.pallas_call(fused_kernel, out_shape=jax.ShapeDtypeStruct((PIECE, HQ *...  59.3 us
    unnamed x1, local copies, waits for them, and re-layouts  2.06 us

profile of v3, /device:TPU:1, one launch (start us, length us, event | category | flops | bytes accessed | tf_op | source)
XLA Modules:
  0.0 61.4 jit_solution(16207888833282564504)
XLA Ops:
  0.0 59.3 %span_attention.1 = bf16[128,3072]{1,0:T(8,128)(2,1)} custom-call(f32[8,24]{1,0:T(8,128)} %temps.1, s32[32]{0:T(128)} %levels.1, s32[4,32]{1,0:T(4,128)} %bitcast.1, s32[32]{0:T(128)} %counts.1, bf16[128,3072]{1,0:T(8,128)(2,1)} %q_ref.1, bf16[128,512]{1,0:T(8,128)(2,1)} %k_ref.1, bf16[128,512]{1,0:T(8,128)(2,1)} %v_ref.1), custom_call_target="tpu_custom_call" | custom-call | tf_op jit(solution)/shard_map/span_attention/pallas_call | solution.py:342
  59.3 2.1 %copy.9 = bf16[128,3072]{1,0:T(8,128)(2,1)} copy(bf16[128,3072]{1,0:T(8,128)(2,1)} %span_attention.1) | data formatting | bytes 1572864

commit v4 on v3

--- a/solution.py
+++ b/solution.py
@@ -18,6 +18,9 @@
 SLOTS = 5
 EARLY = 2
 CHUNK = 256
+PARTS = TOK // CHUNK
+PIECES = GROUP * PARTS
+SPREAD = (1,) * 12
 MESH = pl.DeviceIdType.MESH
 
 
@@ -188,10 +191,12 @@
             preferred_element_type=jnp.float32,
         )
 
-    def early(piece):
-        head, part = piece // (TOK // CHUNK), piece % (TOK // CHUNK)
+    def early_scores(piece):
+        return scores_of(piece // PARTS, piece % PARTS, 0, EARLY)
+
+    def early(piece, scores):
+        head, part = piece // PARTS, piece % PARTS
         rows = pl.ds(part * CHUNK, CHUNK)
-        scores = scores_of(head, part, 0, EARLY)
         top = jnp.max(scores, axis=1, keepdims=True)
         weight = jnp.exp2((scores - top) * scale_of(head)).astype(jnp.bfloat16)
         top_ref[head, rows, :] = jnp.broadcast_to(top, (CHUNK, HD))
@@ -199,10 +204,13 @@
             weight, vx[pl.ds(0, EARLY * TOK), :], preferred_element_type=jnp.float32
         )
 
-    def late(head, part):
+    def late_scores(piece):
+        return scores_of(piece // PARTS, piece % PARTS, EARLY, SLOTS)
+
+    def late(piece, scores):
+        head, part = piece // PARTS, piece % PARTS
         rows = pl.ds(part * CHUNK, CHUNK)
         scale = scale_of(head)
-        scores = scores_of(head, part, EARLY, SLOTS)
         before = top_ref[head, rows, 0:1]
         top = jnp.maximum(before, jnp.max(scores, axis=1, keepdims=True))
         weight = jnp.exp2((scores - top) * scale).astype(jnp.bfloat16)
@@ -263,9 +271,14 @@
     prepare(1, lax.rem(span + 31, 32), span > 0)
     steps = [functools.partial(hop, kv, da) for da in (1, 2) for kv in (0, 1)]
     steps += [functools.partial(last_hop, kv, da) for da in (0, -1, 1, 2) for kv in (0, 1)]
-    for piece, step in enumerate(steps):
+    piece = 0
+    scores = early_scores(0)
+    for step, share in zip(steps, SPREAD):
         step()
-        early(piece)
+        for _ in range(share):
+            ahead = early_scores(piece + 1) if piece + 1 < PIECES else None
+            early(piece, scores)
+            piece, scores = piece + 1, ahead
     for kv in (0, 1):
         for block in range(16):
 
@@ -293,8 +306,8 @@
     def kept(piece):
         return (t == piece) & (yl == core)
 
-    def send_out(head):
-        for piece in range(4):
+    def send_out(head, part):
+        for piece in (2 * part, 2 * part + 1):
 
             @pl.when(kept(piece))
             def _():
@@ -308,11 +321,13 @@
             def _():
                 out_copy(head, piece).start()
 
-    for head in range(GROUP):
-        for part in range(TOK // CHUNK):
-            late(head, part)
-            if head > 0 and part == 0:
-                send_out(head - 1)
+    scores = late_scores(0)
+    for piece in range(PIECES):
+        ahead = late_scores(piece + 1) if piece + 1 < PIECES else None
+        late(piece, scores)
+        scores = ahead
+        if piece > 0:
+            send_out((piece - 1) // PARTS, (piece - 1) % PARTS)
     for kind in range(3):
         for head in range(KVH):
 
@@ -322,7 +337,7 @@
 
     for copy in started + paired:
         copy.wait_send()
-    send_out(GROUP - 1)
+    send_out(GROUP - 1, PARTS - 1)
     for role in range(KVH):
         for head in range(GROUP):
             spot = out_ref.at[:, out_columns(role, head)]

time: 61.5 us -> 57.6 us (0.937)
  Pallas kernels: 59.3 us -> 55.3 us
    pallas_call x1, Pallas kernels: 59.3 us -> 55.3 us  [per_device(): pl.pallas_call(fused_kernel, out_shape=jax.ShapeDtypeStruct((PIECE, HQ *...]
where the time goes in v4:
time: 57.6 us; the launch traced here: 57.4 us
  Pallas kernels  55.3 us (96%)
  local copies, waits for them, and re-layouts  2.06 us (4%)
    pallas_call x1, Pallas kernels, per_device(): pl.pallas_call(fused_kernel, out_shape=jax.ShapeDtypeStruct((PIECE, HQ *...  55.3 us
    unnamed x1, local copies, waits for them, and re-layouts  2.06 us

profile of v4, /device:TPU:1, one launch (start us, length us, event | category | flops | bytes accessed | tf_op | source)
XLA Modules:
  0.0 57.4 jit_solution(5135004006217613762)
XLA Ops:
  0.0 55.3 %span_attention.1 = bf16[128,3072]{1,0:T(8,128)(2,1)} custom-call(f32[8,24]{1,0:T(8,128)} %temps.1, s32[32]{0:T(128)} %levels.1, s32[4,32]{1,0:T(4,128)} %bitcast.1, s32[32]{0:T(128)} %counts.1, bf16[128,3072]{1,0:T(8,128)(2,1)} %q_ref.1, bf16[128,512]{1,0:T(8,128)(2,1)} %k_ref.1, bf16[128,512]{1,0:T(8,128)(2,1)} %v_ref.1), custom_call_target="tpu_custom_call" | custom-call | tf_op jit(solution)/shard_map/span_attention/pallas_call | solution.py:357
  55.3 2.1 %copy.9 = bf16[128,3072]{1,0:T(8,128)(2,1)} copy(bf16[128,3072]{1,0:T(8,128)(2,1)} %span_attention.1) | data formatting | bytes 1572864

commit v5 on v4

--- a/solution.py
+++ b/solution.py
@@ -17,10 +17,10 @@
 PIECE = 128
 SLOTS = 5
 EARLY = 2
-CHUNK = 256
+CHUNK = 512
 PARTS = TOK // CHUNK
 PIECES = GROUP * PARTS
-SPREAD = (1,) * 12
+SPREAD = (1,) * GROUP + (0,) * 6
 MESH = pl.DeviceIdType.MESH
 
 
@@ -95,7 +95,7 @@
             sources[kind].at[:, pl.ds(head * width, width)], landing(kind, yl, t), col_recv.at[kind, t]
         )
 
-    for kind in range(3):
+    def scatter(kind):
         for head in range(KVH):
             mine = (y == head) & (core == yl)
 
@@ -106,6 +106,9 @@
             @pl.when(jnp.logical_not(mine))
             def _():
                 column_copy(kind, head).start()
+
+    scatter(0)
+    scatter(1)
 
     def await_piece(kind, piece):
         spot = landing(kind, core, piece)
@@ -228,12 +231,27 @@
                 for step in (1, -1):
                     send(kv, 0, 0, half, leg, step)
         pair(kv, 0, 0)
+    scatter(2)
+
+    def hop(kv, da):
+        for half in (0, 1):
+            for db in (-1, 1):
+                arrive(kv, da, db, half)
+                if half == (db + 1) // 2:
+                    send(kv, da, db, half, 1, -db)
+        pair(kv, da, -1)
+        pair(kv, da, 1)
+
     for kv in (0, 1):
         for half in (0, 1):
             for da in (-1, 1):
                 arrive(kv, da, 0, half)
                 if half == (da + 1) // 2:
                     send(kv, da, 0, half, 0, -da)
+        hop(kv, 0)
+    for kv in (0, 1):
+        for half in (0, 1):
+            for da in (-1, 1):
                 for step in (1, -1):
                     send(kv, da, 0, half, 1, step)
         pair(kv, -1, 0)
@@ -248,23 +266,13 @@
     for piece in range(4):
         await_piece(2, piece)
 
-    def hop(kv, da):
-        for half in (0, 1):
-            for db in (-1, 1):
-                arrive(kv, da, db, half)
-                if half == (db + 1) // 2:
-                    send(kv, da, db, half, 1, -db)
-        pair(kv, da, -1)
-        pair(kv, da, 1)
-
     def last_hop(kv, da):
         arrive(kv, da, 2, 0)
         arrive(kv, da, 2, 1)
         pair(kv, da, 2)
 
-    for da in (0, -1):
-        for kv in (0, 1):
-            hop(kv, da)
+    for kv in (0, 1):
+        hop(kv, -1)
     near = lax.rem(column + core + 15, 16)
     for kv in (0, 1):
         await_pair(kv, near)
@@ -307,7 +315,7 @@
         return (t == piece) & (yl == core)
 
     def send_out(head, part):
-        for piece in (2 * part, 2 * part + 1):
+        for piece in range(part * 4 // PARTS, (part + 1) * 4 // PARTS):
 
             @pl.when(kept(piece))
             def _():

time: 57.6 us -> 55.9 us (0.970)
  Pallas kernels: 55.3 us -> 53.6 us
    pallas_call x1, Pallas kernels: 55.3 us -> 53.6 us  [per_device(): pl.pallas_call(fused_kernel, out_shape=jax.ShapeDtypeStruct((PIECE, HQ *...]
where the time goes in v5:
time: 55.9 us; the launch traced here: 55.6 us
  Pallas kernels  53.6 us (96%)
  local copies, waits for them, and re-layouts  2.06 us (4%)
    pallas_call x1, Pallas kernels, per_device(): pl.pallas_call(fused_kernel, out_shape=jax.ShapeDtypeStruct((PIECE, HQ *...  53.6 us
    unnamed x1, local copies, waits for them, and re-layouts  2.06 us

profile of v5, /device:TPU:1, one launch (start us, length us, event | category | flops | bytes accessed | tf_op | source)
XLA Modules:
  0.0 55.6 jit_solution(16389434502001300266)
XLA Ops:
  0.0 53.6 %span_attention.1 = bf16[128,3072]{1,0:T(8,128)(2,1)} custom-call(f32[8,24]{1,0:T(8,128)} %temps.1, s32[32]{0:T(128)} %levels.1, s32[4,32]{1,0:T(4,128)} %bitcast.1, s32[32]{0:T(128)} %counts.1, bf16[128,3072]{1,0:T(8,128)(2,1)} %q_ref.1, bf16[128,512]{1,0:T(8,128)(2,1)} %k_ref.1, bf16[128,512]{1,0:T(8,128)(2,1)} %v_ref.1), custom_call_target="tpu_custom_call" | custom-call | tf_op jit(solution)/shard_map/span_attention/pallas_call | solution.py:365
  53.6 2.1 %copy.9 = bf16[128,3072]{1,0:T(8,128)(2,1)} copy(bf16[128,3072]{1,0:T(8,128)(2,1)} %span_attention.1) | data formatting | bytes 1572864

commit v6 on v5

--- a/solution.py
+++ b/solution.py
@@ -20,6 +20,9 @@
 CHUNK = 512
 PARTS = TOK // CHUNK
 PIECES = GROUP * PARTS
+LATE_CHUNK = 256
+LATE_PARTS = TOK // LATE_CHUNK
+LATE_PIECES = GROUP * LATE_PARTS
 SPREAD = (1,) * GROUP + (0,) * 6
 MESH = pl.DeviceIdType.MESH
 
@@ -186,16 +189,16 @@
     def scale_of(head):
         return temps[level, y * GROUP + head] * (math.log2(math.e) / math.sqrt(HD))
 
-    def scores_of(head, part, low, high):
+    def scores_of(head, part, low, high, chunk):
         return lax.dot_general(
-            qa_ref[pl.ds(part * CHUNK, CHUNK), pl.ds(head * HD, HD)],
+            qa_ref[pl.ds(part * chunk, chunk), pl.ds(head * HD, HD)],
             kx[pl.ds(low * TOK, (high - low) * TOK), :],
             (((1,), (1,)), ((), ())),
             preferred_element_type=jnp.float32,
         )
 
     def early_scores(piece):
-        return scores_of(piece // PARTS, piece % PARTS, 0, EARLY)
+        return scores_of(piece // PARTS, piece % PARTS, 0, EARLY, CHUNK)
 
     def early(piece, scores):
         head, part = piece // PARTS, piece % PARTS
@@ -208,11 +211,11 @@
         )
 
     def late_scores(piece):
-        return scores_of(piece // PARTS, piece % PARTS, EARLY, SLOTS)
+        return scores_of(piece // LATE_PARTS, piece % LATE_PARTS, EARLY, SLOTS, LATE_CHUNK)
 
     def late(piece, scores):
-        head, part = piece // PARTS, piece % PARTS
-        rows = pl.ds(part * CHUNK, CHUNK)
+        head, part = piece // LATE_PARTS, piece % LATE_PARTS
+        rows = pl.ds(part * LATE_CHUNK, LATE_CHUNK)
         scale = scale_of(head)
         before = top_ref[head, rows, 0:1]
         top = jnp.maximum(before, jnp.max(scores, axis=1, keepdims=True))
@@ -315,7 +318,7 @@
         return (t == piece) & (yl == core)
 
     def send_out(head, part):
-        for piece in range(part * 4 // PARTS, (part + 1) * 4 // PARTS):
+        for piece in range(part * 4 // LATE_PARTS, (part + 1) * 4 // LATE_PARTS):
 
             @pl.when(kept(piece))
             def _():
@@ -330,12 +333,12 @@
                 out_copy(head, piece).start()
 
     scores = late_scores(0)
-    for piece in range(PIECES):
-        ahead = late_scores(piece + 1) if piece + 1 < PIECES else None
+    for piece in range(LATE_PIECES):
+        ahead = late_scores(piece + 1) if piece + 1 < LATE_PIECES else None
         late(piece, scores)
         scores = ahead
         if piece > 0:
-            send_out((piece - 1) // PARTS, (piece - 1) % PARTS)
+            send_out((piece - 1) // LATE_PARTS, (piece - 1) % LATE_PARTS)
     for kind in range(3):
         for head in range(KVH):
 
@@ -345,7 +348,7 @@
 
     for copy in started + paired:
         copy.wait_send()
-    send_out(GROUP - 1, PARTS - 1)
+    send_out(GROUP - 1, LATE_PARTS - 1)
     for role in range(KVH):
         for head in range(GROUP):
             spot = out_ref.at[:, out_columns(role, head)]

time: 55.9 us -> 55.9 us (level)
  no operation moved by 1% of the time
where the time goes in v6:
time: 55.9 us; the launch traced here: 55.6 us
  Pallas kernels  53.6 us (96%)
  local copies, waits for them, and re-layouts  2.06 us (4%)
    pallas_call x1, Pallas kernels, per_device(): pl.pallas_call(fused_kernel, out_shape=jax.ShapeDtypeStruct((PIECE, HQ *...  53.6 us
    unnamed x1, local copies, waits for them, and re-layouts  2.06 us

profile of v6, /device:TPU:1, one launch (start us, length us, event | category | flops | bytes accessed | tf_op | source)
XLA Modules:
  0.0 55.6 jit_solution(11888452511552748203)
XLA Ops:
  0.0 53.6 %span_attention.1 = bf16[128,3072]{1,0:T(8,128)(2,1)} custom-call(f32[8,24]{1,0:T(8,128)} %temps.1, s32[32]{0:T(128)} %levels.1, s32[4,32]{1,0:T(4,128)} %bitcast.1, s32[32]{0:T(128)} %counts.1, bf16[128,3072]{1,0:T(8,128)(2,1)} %q_ref.1, bf16[128,512]{1,0:T(8,128)(2,1)} %k_ref.1, bf16[128,512]{1,0:T(8,128)(2,1)} %v_ref.1), custom_call_target="tpu_custom_call" | custom-call | tf_op jit(solution)/shard_map/span_attention/pallas_call | solution.py:368
  53.6 2.1 %copy.9 = bf16[128,3072]{1,0:T(8,128)(2,1)} copy(bf16[128,3072]{1,0:T(8,128)(2,1)} %span_attention.1) | data formatting | bytes 1572864
